TPU v7x, 256 devices: a whole 4x4x8 slice. The times are simulated.
256 devices in a mesh: rows: 16 (over x, y_lo, core), cols: 16 (over z, y_hi).
Axes of the slice: x: 4, y: 4 (y_hi: 2, y_lo: 2; y = y_hi * 2 + y_lo), z: 8, core: 2. Of those that a mesh axis runs over, the one named last changes fastest.
Arguments:
- unary: float32 [21, 256, 2048], P(None, 'rows', 'cols'), may hold values from -8 to 300
- features: bfloat16 [64, 256, 2048], P(None, 'rows', 'cols'), may hold values from -9 to 9
- compat: float32 [21, 21], replicated, may hold values from -6 to 6
- grad_output: float32 [21, 256, 2048], P(None, 'rows', 'cols'), may hold values from -6 to 6
Outputs:
- unary_grad: float32 [21, 256, 2048], P(None, 'rows', 'cols')
- feature_grad: float32 [64, 256, 2048], P(None, 'rows', 'cols')
- compat_grad: float32 [21, 21], replicated
All inputs are finite; a program needn't handle non-finite values.
Results may differ from a plain program's by a relative error of at most 0.0003.
Values may be sent and summed in bfloat16 or wider, within the bound.
A program may use at most 128 MiB of HBM per device.

v0:
```python
import math
import jax
import jax.numpy as jnp
from jax import lax
from jax.sharding import PartitionSpec as P

ITERS = 2
THETA_PIXELS = 3.0
WINDOW_OFFSETS = [
    (row_step, col_step)
    for row_step in range(-3, 4)
    for col_step in range(-3, 4)
    if row_step != 0 or col_step != 0
]


def with_halo(block, sides, width):
    for axis, dim in sides:
        count = lax.axis_size(axis)
        forward = [(i, i + 1) for i in range(count - 1)]
        backward = [(target, source) for source, target in forward]
        low = lax.ppermute(
            lax.slice_in_dim(block, block.shape[dim] - width, None, axis=dim), axis, forward
        )
        high = lax.ppermute(lax.slice_in_dim(block, 0, width, axis=dim), axis, backward)
        block = jnp.concatenate([low, block, high], axis=dim)
    return block


def spatial_weight(row_step, col_step):
    return math.exp(
        -(row_step * row_step + col_step * col_step) / (2.0 * THETA_PIXELS * THETA_PIXELS)
    )


def shifted_view(padded, row_step, col_step, height, width_cells):
    return padded[
        :, 3 + row_step : 3 + row_step + height, 3 + col_step : 3 + col_step + width_cells
    ]


def affinity(padded_features):
    height = padded_features.shape[1] - 6
    width_cells = padded_features.shape[2] - 6
    center = shifted_view(padded_features, 0, 0, height, width_cells).astype(jnp.float32)
    factor = 1.0 / (2.0 * padded_features.shape[0])
    layers = []
    for row_step, col_step in WINDOW_OFFSETS:
        shifted = shifted_view(padded_features, row_step, col_step, height, width_cells).astype(
            jnp.float32
        )
        distance = jnp.sum((shifted - center) * (shifted - center), axis=0)
        layers.append(spatial_weight(row_step, col_step) * jnp.exp(-distance * factor))
    return jnp.stack(layers)


def message(kernel, padded):
    height = kernel.shape[1]
    width_cells = kernel.shape[2]
    total = jnp.zeros((padded.shape[0], height, width_cells), jnp.float32)
    for number, (row_step, col_step) in enumerate(WINDOW_OFFSETS):
        total = total + kernel[number][None] * shifted_view(
            padded, row_step, col_step, height, width_cells
        )
    return total


def pair_terms(grad_padded, prob_padded):
    height = grad_padded.shape[1] - 6
    width_cells = grad_padded.shape[2] - 6
    grad_center = shifted_view(grad_padded, 0, 0, height, width_cells)
    prob_center = shifted_view(prob_padded, 0, 0, height, width_cells)
    layers = []
    for row_step, col_step in WINDOW_OFFSETS:
        prob_shift = shifted_view(prob_padded, row_step, col_step, height, width_cells)
        grad_shift = shifted_view(grad_padded, row_step, col_step, height, width_cells)
        layers.append(jnp.sum(grad_center * prob_shift + grad_shift * prob_center, axis=0))
    return jnp.stack(layers)


def feature_term(coefs, kernel, padded_features):
    height = kernel.shape[1]
    width_cells = kernel.shape[2]
    center = shifted_view(padded_features, 0, 0, height, width_cells).astype(jnp.float32)
    factor = 1.0 / padded_features.shape[0]
    total = jnp.zeros(center.shape, jnp.float32)
    for number, (row_step, col_step) in enumerate(WINDOW_OFFSETS):
        shifted = shifted_view(padded_features, row_step, col_step, height, width_cells).astype(
            jnp.float32
        )
        weight_map = coefs[number] * kernel[number] * factor
        total = total + weight_map[None] * (shifted - center)
    return total


def mix(compat, values):
    return jnp.einsum("cd,dhw->chw", compat, values, precision=lax.Precision.HIGHEST)


def mix_back(compat, values):
    return jnp.einsum("cd,chw->dhw", compat, values, precision=lax.Precision.HIGHEST)


def outer_sum(left, right):
    return jnp.einsum("chw,dhw->cd", left, right, precision=lax.Precision.HIGHEST)


def softmax_grad(prob, cotangent):
    return prob * (cotangent - jnp.sum(cotangent * prob, axis=0, keepdims=True))


def on_device(unary, features, compat, grad_output):
    height = unary.shape[1]
    width_cells = unary.shape[2]
    total_pixels = height * lax.axis_size("rows") * width_cells * lax.axis_size("cols")
    reach = 0
    feat_wide = with_halo(features, (("rows", 1), ("cols", 2)), 3)
    cotangent = grad_output
    start_prob = jax.nn.softmax(unary, axis=0)
    kern_store = affinity(feat_wide)

    def kernel_at():
        return kern_store

    prob_list = [start_prob]
    pad_list = [reach]
    wide_list = []
    message_list = []
    for step in range(ITERS):
        current = prob_list[-1]
        prob_wide = with_halo(current, (("rows", 1), ("cols", 2)), 3)
        wide_pad = 3
        wide_list.append((prob_wide, wide_pad))
        out_pad = wide_pad - 3
        message_out = message(kernel_at(), prob_wide)
        message_list.append(message_out)
        logits = unary - mix(compat, message_out)
        next_prob = jax.nn.softmax(logits, axis=0)
        prob_list.append(next_prob)
        pad_list.append(out_pad)
    unary_sum = jnp.zeros(unary.shape, jnp.float32)
    compat_sum = jnp.zeros(compat.shape, jnp.float32)
    coefs = jnp.zeros((len(WINDOW_OFFSETS), height, width_cells), jnp.float32)
    for step in reversed(range(ITERS)):
        later_prob = prob_list[step + 1]
        logit_grad = softmax_grad(later_prob, cotangent)
        unary_sum = unary_sum + logit_grad
        compat_sum = compat_sum - outer_sum(logit_grad, message_list[step])
        msg_grad = -mix_back(compat, logit_grad)
        grad_wide = with_halo(msg_grad, (("rows", 1), ("cols", 2)), 3)
        cotangent = message(kernel_at(), grad_wide)
        prob_wide, wide_pad = wide_list[step]
        coefs = coefs + pair_terms(grad_wide, prob_wide)
    unary_grad = unary_sum + softmax_grad(prob_list[0], cotangent)
    feature_grad = feature_term(coefs, kernel_at(), feat_wide)
    compat_grad = lax.psum(compat_sum, ("rows", "cols")) / math.sqrt(total_pixels)
    return (unary_grad, feature_grad, compat_grad)


def solution(mesh):
    placed = (P(None, "rows", "cols"), P(None, "rows", "cols"), P(), P(None, "rows", "cols"))
    return jax.shard_map(
        on_device,
        mesh=mesh,
        in_specs=placed,
        out_specs=(P(None, "rows", "cols"), P(None, "rows", "cols"), P()),
        check_vma=False,
    )
```

profile of v0, /device:TPU:33, one launch (start us, length us, event | category | flops | bytes accessed | tf_op | source)
XLA Modules:
  0.0 314.2 jit_solution(16345287022579159694)
XLA Ops:
  3.7 3.8 %collective-permute-start.3 = (f32[21,3,128]{2,0,1:T(8,128)S(1)}, f32[21,3,128]{2,0,1:T(8,128)S(1)}, u32[]{:S(2)}, u32[]{:S(2)}) collective-permute-start(f32[21,3,128]{2,0,1:T(8,128)S(1)} %get-tuple-element.238), channel_id=1, source_target_pairs={{0,16},{16,32},{32,48},{48,64},{64,80},{80,96},{96,112},{112,128},... | collective-permute-start | bytes 96776 | tf_op jit(solution)/shard_map/ppermute | solution.py:22
  9.5 3.6 %collective-permute-start = (bf16[64,3,128]{2,1,0:T(4,128)(2,1)S(1)}, bf16[64,3,128]{2,1,0:T(4,128)(2,1)S(1)}, u32[]{:S(2)}, u32[]{:S(2)}) collective-permute-start(bf16[64,3,128]{2,1,0:T(4,128)(2,1)S(1)} %get-tuple-element.229), channel_id=1, source_target_pairs={{0,16},{16,32},{32,48},{48,64},{64,80},{80,96},{96,112},{112,128},... | collective-permute-start | bytes 147464 | tf_op jit(solution)/shard_map/ppermute | solution.py:22
  15.2 4.5 %collective-permute-start.5 = (f32[21,22,3]{2,0,1:T(8,128)S(1)}, f32[21,22,3]{2,0,1:T(8,128)S(1)}, u32[]{:S(2)}, u32[]{:S(2)}) collective-permute-start(f32[21,22,3]{2,0,1:T(8,128)S(1)} %get-tuple-element.227), channel_id=1, source_target_pairs={{0,1},{1,2},{2,3},{3,4},{4,5},{5,6},{6,7},{7,8},{8,9},{9,10},{10,1... | collective-permute-start | bytes 16640 | tf_op jit(solution)/shard_map/ppermute | solution.py:22
  19.8 3.2 %collective-permute-start.7 = (f32[21,22,3]{2,0,1:T(8,128)S(1)}, f32[21,22,3]{2,0,1:T(8,128)S(1)}, u32[]{:S(2)}, u32[]{:S(2)}) collective-permute-start(f32[21,22,3]{2,0,1:T(8,128)S(1)} %get-tuple-element.228), channel_id=1, source_target_pairs={{1,0},{2,1},{3,2},{4,3},{5,4},{6,5},{7,6},{8,7},{9,8},{10,9},{11,1... | collective-permute-start | bytes 16640 | tf_op jit(solution)/shard_map/ppermute | solution.py:25
  23.0 8.2 %collective-permute-done.5 = f32[21,22,3]{2,0,1:T(8,128)S(1)} collective-permute-done((f32[21,22,3]{2,0,1:T(8,128)S(1)}, f32[21,22,3]{2,0,1:T(8,128)S(1)}, u32[]{:S(2)}, u32[]{:S(2)}) %collective-permute-start.5) | collective-permute-done | bytes 5576 | tf_op jit(solution)/shard_map/ppermute | solution.py:22
  36.7 3.8 %collective-permute-start.2 = (bf16[64,22,3]{2,1,0:T(8,128)(2,1)S(1)}, bf16[64,22,3]{2,1,0:T(8,128)(2,1)S(1)}, u32[]{:S(2)}, u32[]{:S(2)}) collective-permute-start(bf16[64,22,3]{2,1,0:T(8,128)(2,1)S(1)} %get-tuple-element.212), channel_id=1, source_target_pairs={{0,1},{1,2},{2,3},{3,4},{4,5},{5,6},{6,7},{7,8},{8,9},{9,10},{10,1... | collective-permute-start | bytes 25352 | tf_op jit(solution)/shard_map/ppermute | solution.py:22
  40.5 15.3 %collective-permute-done.6 = bf16[64,22,3]{2,1,0:T(8,128)(2,1)S(1)} collective-permute-done((bf16[64,22,3]{2,1,0:T(8,128)(2,1)S(1)}, bf16[64,22,3]{2,1,0:T(8,128)(2,1)S(1)}, u32[]{:S(2)}, u32[]{:S(2)}) %collective-permute-start.6) | collective-permute-done | bytes 8480 | tf_op jit(solution)/shard_map/ppermute | solution.py:25
  83.4 5.8 %collective-permute-start.8 = (f32[21,3,128]{2,0,1:T(8,128)S(1)}, f32[21,3,128]{2,0,1:T(8,128)S(1)}, u32[]{:S(2)}, u32[]{:S(2)}) collective-permute-start(f32[21,3,128]{2,0,1:T(8,128)S(1)} %get-tuple-element.236), channel_id=1, source_target_pairs={{0,16},{16,32},{32,48},{48,64},{64,80},{80,96},{96,112},{112,128},... | collective-permute-start | bytes 96776 | tf_op jit(solution)/shard_map/ppermute | solution.py:22
  91.1 3.3 %collective-permute-done.9 = f32[21,3,128]{2,0,1:T(8,128)S(1)} collective-permute-done((f32[21,3,128]{2,0,1:T(8,128)S(1)}, f32[21,3,128]{2,0,1:T(8,128)S(1)}, u32[]{:S(2)}, u32[]{:S(2)}) %collective-permute-start.9) | collective-permute-done | bytes 32288 | tf_op jit(solution)/shard_map/ppermute | solution.py:25
  94.6 4.8 %collective-permute-start.10 = (f32[21,22,3]{2,0,1:T(8,128)S(1)}, f32[21,22,3]{2,0,1:T(8,128)S(1)}, u32[]{:S(2)}, u32[]{:S(2)}) collective-permute-start(f32[21,22,3]{2,0,1:T(8,128)S(1)} %get-tuple-element.223), channel_id=1, source_target_pairs={{0,1},{1,2},{2,3},{3,4},{4,5},{5,6},{6,7},{7,8},{8,9},{9,10},{10,1... | collective-permute-start | bytes 16640 | tf_op jit(solution)/shard_map/ppermute | solution.py:22
  102.5 7.3 %collective-permute-done.10 = f32[21,22,3]{2,0,1:T(8,128)S(1)} collective-permute-done((f32[21,22,3]{2,0,1:T(8,128)S(1)}, f32[21,22,3]{2,0,1:T(8,128)S(1)}, u32[]{:S(2)}, u32[]{:S(2)}) %collective-permute-start.10) | collective-permute-done | bytes 5576 | tf_op jit(solution)/shard_map/ppermute | solution.py:22
  118.5 4.6 %collective-permute-start.12 = (f32[21,3,128]{2,0,1:T(8,128)S(1)}, f32[21,3,128]{2,0,1:T(8,128)S(1)}, u32[]{:S(2)}, u32[]{:S(2)}) collective-permute-start(f32[21,3,128]{2,0,1:T(8,128)S(1)} %get-tuple-element.234), channel_id=1, source_target_pairs={{0,16},{16,32},{32,48},{48,64},{64,80},{80,96},{96,112},{112,128},... | collective-permute-start | bytes 96776 | tf_op jit(solution)/shard_map/ppermute | solution.py:22
  125.0 3.3 %collective-permute-done.13 = f32[21,3,128]{2,0,1:T(8,128)S(1)} collective-permute-done((f32[21,3,128]{2,0,1:T(8,128)S(1)}, f32[21,3,128]{2,0,1:T(8,128)S(1)}, u32[]{:S(2)}, u32[]{:S(2)}) %collective-permute-start.13) | collective-permute-done | bytes 32288 | tf_op jit(solution)/shard_map/ppermute | solution.py:25
  128.5 3.9 %collective-permute-start.14 = (f32[21,22,3]{2,0,1:T(8,128)S(1)}, f32[21,22,3]{2,0,1:T(8,128)S(1)}, u32[]{:S(2)}, u32[]{:S(2)}) collective-permute-start(f32[21,22,3]{2,0,1:T(8,128)S(1)} %get-tuple-element.219), channel_id=1, source_target_pairs={{0,1},{1,2},{2,3},{3,4},{4,5},{5,6},{6,7},{7,8},{8,9},{9,10},{10,1... | collective-permute-start | bytes 16640 | tf_op jit(solution)/shard_map/ppermute | solution.py:22
  132.4 3.8 %collective-permute-start.15 = (f32[21,22,3]{2,0,1:T(8,128)S(1)}, f32[21,22,3]{2,0,1:T(8,128)S(1)}, u32[]{:S(2)}, u32[]{:S(2)}) collective-permute-start(f32[21,22,3]{2,0,1:T(8,128)S(1)} %get-tuple-element.220), channel_id=1, source_target_pairs={{1,0},{2,1},{3,2},{4,3},{5,4},{6,5},{7,6},{8,7},{9,8},{10,9},{11,1... | collective-permute-start | bytes 16640 | tf_op jit(solution)/shard_map/ppermute | solution.py:25
  136.9 5.8 %collective-permute-done.14 = f32[21,22,3]{2,0,1:T(8,128)S(1)} collective-permute-done((f32[21,22,3]{2,0,1:T(8,128)S(1)}, f32[21,22,3]{2,0,1:T(8,128)S(1)}, u32[]{:S(2)}, u32[]{:S(2)}) %collective-permute-start.14) | collective-permute-done | bytes 5576 | tf_op jit(solution)/shard_map/ppermute | solution.py:22
  152.1 4.4 %add_reduce_fusion.48 = (f32[16,128]{1,0:T(8,128)}, f32[16,128]{1,0:T(8,128)}, f32[16,128]{1,0:T(8,128)}, f32[16,128]{1,0:T(8,128)}, f32[16,128]{1,0:T(8,128)}, ...) fusion(f32[21,16,128]{2,0,1:T(8,128)S(1)} %fusion.11, ...), kind=kLoop, calls=%fused_computation.349 | loop fusion | flops 5830656 | bytes 9657344 | tf_op jit(solution)/shard_map/reduce_sum | solution.py:77
  159.8 81.1 %psum.7 = f32[21,21]{1,0:T(8,128)S(1)} all-reduce(f32[21,21]{1,0:T(8,128)S(1)} %fusion.15), channel_id=1, replica_groups=mesh['rows'=16,'cols'=16] {'rows','cols'}, use_global_device_ids=true, to_apply=%region_153.0 | all-reduce | flops 441 | bytes 3528 | tf_op jit(solution)/shard_map/psum | solution.py:156
  257.8 3.8 %collective-permute-start.18 = (f32[21,22,3]{2,0,1:T(8,128)S(1)}, f32[21,22,3]{2,0,1:T(8,128)S(1)}, u32[]{:S(2)}, u32[]{:S(2)}) collective-permute-start(f32[21,22,3]{2,0,1:T(8,128)S(1)} %get-tuple-element.215), channel_id=1, source_target_pairs={{0,1},{1,2},{2,3},{3,4},{4,5},{5,6},{6,7},{7,8},{8,9},{9,10},{10,1... | collective-permute-start | bytes 16640 | tf_op jit(solution)/shard_map/ppermute | solution.py:22
  261.6 4.1 %collective-permute-start.19 = (f32[21,22,3]{2,0,1:T(8,128)S(1)}, f32[21,22,3]{2,0,1:T(8,128)S(1)}, u32[]{:S(2)}, u32[]{:S(2)}) collective-permute-start(f32[21,22,3]{2,0,1:T(8,128)S(1)} %get-tuple-element.216), channel_id=1, source_target_pairs={{1,0},{2,1},{3,2},{4,3},{5,4},{6,5},{7,6},{8,7},{9,8},{10,9},{11,1... | collective-permute-start | bytes 16640 | tf_op jit(solution)/shard_map/ppermute | solution.py:25
  266.0 6.7 %collective-permute-done.18 = f32[21,22,3]{2,0,1:T(8,128)S(1)} collective-permute-done((f32[21,22,3]{2,0,1:T(8,128)S(1)}, f32[21,22,3]{2,0,1:T(8,128)S(1)}, u32[]{:S(2)}, u32[]{:S(2)}) %collective-permute-start.18) | collective-permute-done | bytes 5576 | tf_op jit(solution)/shard_map/ppermute | solution.py:22
  272.7 3.5 %collective-permute-done.19 = f32[21,22,3]{2,0,1:T(8,128)S(1)} collective-permute-done((f32[21,22,3]{2,0,1:T(8,128)S(1)}, f32[21,22,3]{2,0,1:T(8,128)S(1)}, u32[]{:S(2)}, u32[]{:S(2)}) %collective-permute-start.19) | collective-permute-done | bytes 5576 | tf_op jit(solution)/shard_map/ppermute | solution.py:25
  290.9 13.9 %fusion.7 = f32[21,16,128]{2,0,1:T(8,128)S(1)} fusion(f32[21,16,128]{2,0,1:T(8,128)S(1)} %copy-done.10, f32[16,128]{1,0:T(8,128)} %fusion.19, f32[21,16,128]{2,1,0:T(8,128)} %param.7, f32[21,16,128]{2,0,1:T(8,128)} %copy-done.11, f32[16,128]{1,0:T(8,128)} %get-tuple-element.242, f32[16,128]{1,0:T(8,128)S(1)} %copy-done.13, f32[16,128]{1,0:T(8,128)S(1)} %reduce_max.27, ...), kind=kOutput, calls=%fused_computation.55 | output fusion | flops 9205780 | bytes 18972672 | tf_op jit(solution)/shard_map/sub | solution.py:109
  305.9 8.3 %multiply_add_fusion = f32[64,16,128]{2,1,0:T(8,128)} fusion(bf16[64,16,128]{2,1,0:T(8,128)(2,1)S(1)} %copy-done.6, bf16[64,3,128]{2,1,0:T(4,128)(2,1)S(1)} %collective-permute-done, f32[16,128]{1,0:T(8,128)} %get-tuple-element.162, f32[16,128]{1,0:T(8,128)} %get-tuple-element.163, f32[16,128]{1,0:T(8,128)} %get-tuple-element.164, ...), kind=kLoop, calls=%fused_computation.80 | loop fusion | flops 26345472 | bytes 13025280 | tf_op jit(solution)/shard_map/add | solution.py:92
  (516 shorter events, 99.3 us)
Async XLA Ops:
  3.7 11.4 %collective-permute-start.3 = (f32[21,3,128]{2,0,1:T(8,128)S(1)}, f32[21,3,128]{2,0,1:T(8,128)S(1)}, u32[]{:S(2)}, u32[]{:S(2)}) collective-permute-start(f32[21,3,128]{2,0,1:T(8,128)S(1)} %get-tuple-element.238), channel_id=1, source_target_pairs={{0,16},{16,32},{32,48},{48,64},{64,80},{80,96},{96,112},{112,128},... | collective-permute-start | bytes 96776 | tf_op jit(solution)/shard_map/ppermute | solution.py:22
  7.5 7.6 %collective-permute-start.4 = (f32[21,3,128]{2,0,1:T(8,128)S(1)}, f32[21,3,128]{2,0,1:T(8,128)S(1)}, u32[]{:S(2)}, u32[]{:S(2)}) collective-permute-start(f32[21,3,128]{2,0,1:T(8,128)S(1)} %get-tuple-element.239), channel_id=1, source_target_pairs={{16,0},{32,16},{48,32},{64,48},{80,64},{96,80},{112,96},{128,112},... | collective-permute-start | bytes 96776 | tf_op jit(solution)/shard_map/ppermute | solution.py:25
  9.5 23.8 %collective-permute-start = (bf16[64,3,128]{2,1,0:T(4,128)(2,1)S(1)}, bf16[64,3,128]{2,1,0:T(4,128)(2,1)S(1)}, u32[]{:S(2)}, u32[]{:S(2)}) collective-permute-start(bf16[64,3,128]{2,1,0:T(4,128)(2,1)S(1)} %get-tuple-element.229), channel_id=1, source_target_pairs={{0,16},{16,32},{32,48},{48,64},{64,80},{80,96},{96,112},{112,128},... | collective-permute-start | bytes 147464 | tf_op jit(solution)/shard_map/ppermute | solution.py:22
  13.1 20.1 %collective-permute-start.1 = (bf16[64,3,128]{2,1,0:T(4,128)(2,1)S(1)}, bf16[64,3,128]{2,1,0:T(4,128)(2,1)S(1)}, u32[]{:S(2)}, u32[]{:S(2)}) collective-permute-start(bf16[64,3,128]{2,1,0:T(4,128)(2,1)S(1)} %get-tuple-element.230), channel_id=1, source_target_pairs={{16,0},{32,16},{48,32},{64,48},{80,64},{96,80},{112,96},{128,112},... | collective-permute-start | bytes 147464 | tf_op jit(solution)/shard_map/ppermute | solution.py:25
  15.2 15.9 %collective-permute-start.5 = (f32[21,22,3]{2,0,1:T(8,128)S(1)}, f32[21,22,3]{2,0,1:T(8,128)S(1)}, u32[]{:S(2)}, u32[]{:S(2)}) collective-permute-start(f32[21,22,3]{2,0,1:T(8,128)S(1)} %get-tuple-element.227), channel_id=1, source_target_pairs={{0,1},{1,2},{2,3},{3,4},{4,5},{5,6},{6,7},{7,8},{8,9},{9,10},{10,1... | collective-permute-start | bytes 16640 | tf_op jit(solution)/shard_map/ppermute | solution.py:22
  19.8 13.3 %collective-permute-start.7 = (f32[21,22,3]{2,0,1:T(8,128)S(1)}, f32[21,22,3]{2,0,1:T(8,128)S(1)}, u32[]{:S(2)}, u32[]{:S(2)}) collective-permute-start(f32[21,22,3]{2,0,1:T(8,128)S(1)} %get-tuple-element.228), channel_id=1, source_target_pairs={{1,0},{2,1},{3,2},{4,3},{5,4},{6,5},{7,6},{8,7},{9,8},{10,9},{11,1... | collective-permute-start | bytes 16640 | tf_op jit(solution)/shard_map/ppermute | solution.py:25
  33.7 22.1 %collective-permute-start.6 = (bf16[64,22,3]{2,1,0:T(8,128)(2,1)S(1)}, bf16[64,22,3]{2,1,0:T(8,128)(2,1)S(1)}, u32[]{:S(2)}, u32[]{:S(2)}) collective-permute-start(bf16[64,22,3]{2,1,0:T(8,128)(2,1)S(1)} %get-tuple-element.211), channel_id=1, source_target_pairs={{1,0},{2,1},{3,2},{4,3},{5,4},{6,5},{7,6},{8,7},{9,8},{10,9},{11,1... | collective-permute-start | bytes 25352 | tf_op jit(solution)/shard_map/ppermute | solution.py:25
  36.7 19.1 %collective-permute-start.2 = (bf16[64,22,3]{2,1,0:T(8,128)(2,1)S(1)}, bf16[64,22,3]{2,1,0:T(8,128)(2,1)S(1)}, u32[]{:S(2)}, u32[]{:S(2)}) collective-permute-start(bf16[64,22,3]{2,1,0:T(8,128)(2,1)S(1)} %get-tuple-element.212), channel_id=1, source_target_pairs={{0,1},{1,2},{2,3},{3,4},{4,5},{5,6},{6,7},{7,8},{8,9},{9,10},{10,1... | collective-permute-start | bytes 25352 | tf_op jit(solution)/shard_map/ppermute | solution.py:22
  83.4 7.7 %collective-permute-start.8 = (f32[21,3,128]{2,0,1:T(8,128)S(1)}, f32[21,3,128]{2,0,1:T(8,128)S(1)}, u32[]{:S(2)}, u32[]{:S(2)}) collective-permute-start(f32[21,3,128]{2,0,1:T(8,128)S(1)} %get-tuple-element.236), channel_id=1, source_target_pairs={{0,16},{16,32},{32,48},{48,64},{64,80},{80,96},{96,112},{112,128},... | collective-permute-start | bytes 96776 | tf_op jit(solution)/shard_map/ppermute | solution.py:22
  89.2 5.3 %collective-permute-start.9 = (f32[21,3,128]{2,0,1:T(8,128)S(1)}, f32[21,3,128]{2,0,1:T(8,128)S(1)}, u32[]{:S(2)}, u32[]{:S(2)}) collective-permute-start(f32[21,3,128]{2,0,1:T(8,128)S(1)} %get-tuple-element.237), channel_id=1, source_target_pairs={{16,0},{32,16},{48,32},{64,48},{80,64},{96,80},{112,96},{128,112},... | collective-permute-start | bytes 96776 | tf_op jit(solution)/shard_map/ppermute | solution.py:25
  94.6 15.2 %collective-permute-start.10 = (f32[21,22,3]{2,0,1:T(8,128)S(1)}, f32[21,22,3]{2,0,1:T(8,128)S(1)}, u32[]{:S(2)}, u32[]{:S(2)}) collective-permute-start(f32[21,22,3]{2,0,1:T(8,128)S(1)} %get-tuple-element.223), channel_id=1, source_target_pairs={{0,1},{1,2},{2,3},{3,4},{4,5},{5,6},{6,7},{7,8},{8,9},{9,10},{10,1... | collective-permute-start | bytes 16640 | tf_op jit(solution)/shard_map/ppermute | solution.py:22
  99.4 12.0 %collective-permute-start.11 = (f32[21,22,3]{2,0,1:T(8,128)S(1)}, f32[21,22,3]{2,0,1:T(8,128)S(1)}, u32[]{:S(2)}, u32[]{:S(2)}) collective-permute-start(f32[21,22,3]{2,0,1:T(8,128)S(1)} %get-tuple-element.224), channel_id=1, source_target_pairs={{1,0},{2,1},{3,2},{4,3},{5,4},{6,5},{7,6},{8,7},{9,8},{10,9},{11,1... | collective-permute-start | bytes 16640 | tf_op jit(solution)/shard_map/ppermute | solution.py:25
  118.5 6.5 %collective-permute-start.12 = (f32[21,3,128]{2,0,1:T(8,128)S(1)}, f32[21,3,128]{2,0,1:T(8,128)S(1)}, u32[]{:S(2)}, u32[]{:S(2)}) collective-permute-start(f32[21,3,128]{2,0,1:T(8,128)S(1)} %get-tuple-element.234), channel_id=1, source_target_pairs={{0,16},{16,32},{32,48},{48,64},{64,80},{80,96},{96,112},{112,128},... | collective-permute-start | bytes 96776 | tf_op jit(solution)/shard_map/ppermute | solution.py:22
  123.0 5.3 %collective-permute-start.13 = (f32[21,3,128]{2,0,1:T(8,128)S(1)}, f32[21,3,128]{2,0,1:T(8,128)S(1)}, u32[]{:S(2)}, u32[]{:S(2)}) collective-permute-start(f32[21,3,128]{2,0,1:T(8,128)S(1)} %get-tuple-element.235), channel_id=1, source_target_pairs={{16,0},{32,16},{48,32},{64,48},{80,64},{96,80},{112,96},{128,112},... | collective-permute-start | bytes 96776 | tf_op jit(solution)/shard_map/ppermute | solution.py:25
  128.5 14.3 %collective-permute-start.14 = (f32[21,22,3]{2,0,1:T(8,128)S(1)}, f32[21,22,3]{2,0,1:T(8,128)S(1)}, u32[]{:S(2)}, u32[]{:S(2)}) collective-permute-start(f32[21,22,3]{2,0,1:T(8,128)S(1)} %get-tuple-element.219), channel_id=1, source_target_pairs={{0,1},{1,2},{2,3},{3,4},{4,5},{5,6},{6,7},{7,8},{8,9},{9,10},{10,1... | collective-permute-start | bytes 16640 | tf_op jit(solution)/shard_map/ppermute | solution.py:22
  132.4 12.9 %collective-permute-start.15 = (f32[21,22,3]{2,0,1:T(8,128)S(1)}, f32[21,22,3]{2,0,1:T(8,128)S(1)}, u32[]{:S(2)}, u32[]{:S(2)}) collective-permute-start(f32[21,22,3]{2,0,1:T(8,128)S(1)} %get-tuple-element.220), channel_id=1, source_target_pairs={{1,0},{2,1},{3,2},{4,3},{5,4},{6,5},{7,6},{8,7},{9,8},{10,9},{11,1... | collective-permute-start | bytes 16640 | tf_op jit(solution)/shard_map/ppermute | solution.py:25
  158.6 98.9 %copy-start.125 = (f32[16,128]{1,0:T(8,128)S(1)}, f32[16,128]{1,0:T(8,128)}, u32[]{:S(2)}) copy-start(f32[16,128]{1,0:T(8,128)} %get-tuple-element.14) | copy-start | bytes 24580
  158.7 98.9 %copy-start.130 = (f32[16,128]{1,0:T(8,128)S(1)}, f32[16,128]{1,0:T(8,128)}, u32[]{:S(2)}) copy-start(f32[16,128]{1,0:T(8,128)} %get-tuple-element.8) | copy-start | bytes 24580
  158.7 98.9 %copy-start.129 = (f32[16,128]{1,0:T(8,128)S(1)}, f32[16,128]{1,0:T(8,128)}, u32[]{:S(2)}) copy-start(f32[16,128]{1,0:T(8,128)} %get-tuple-element.7) | copy-start | bytes 24580
  158.7 98.9 %copy-start.128 = (f32[16,128]{1,0:T(8,128)S(1)}, f32[16,128]{1,0:T(8,128)}, u32[]{:S(2)}) copy-start(f32[16,128]{1,0:T(8,128)} %get-tuple-element.6) | copy-start | bytes 24580
  241.5 16.1 %collective-permute-start.16 = (f32[21,3,128]{2,0,1:T(8,128)S(1)}, f32[21,3,128]{2,0,1:T(8,128)S(1)}, u32[]{:S(2)}, u32[]{:S(2)}) collective-permute-start(f32[21,3,128]{2,0,1:T(8,128)S(1)} %get-tuple-element.232), channel_id=1, source_target_pairs={{0,16},{16,32},{32,48},{48,64},{64,80},{80,96},{96,112},{112,128},... | collective-permute-start | bytes 96776 | tf_op jit(solution)/shard_map/ppermute | solution.py:22
  243.5 14.2 %collective-permute-start.17 = (f32[21,3,128]{2,0,1:T(8,128)S(1)}, f32[21,3,128]{2,0,1:T(8,128)S(1)}, u32[]{:S(2)}, u32[]{:S(2)}) collective-permute-start(f32[21,3,128]{2,0,1:T(8,128)S(1)} %get-tuple-element.233), channel_id=1, source_target_pairs={{16,0},{32,16},{48,32},{64,48},{80,64},{96,80},{112,96},{128,112},... | collective-permute-start | bytes 96776 | tf_op jit(solution)/shard_map/ppermute | solution.py:25
  257.8 14.9 %collective-permute-start.18 = (f32[21,22,3]{2,0,1:T(8,128)S(1)}, f32[21,22,3]{2,0,1:T(8,128)S(1)}, u32[]{:S(2)}, u32[]{:S(2)}) collective-permute-start(f32[21,22,3]{2,0,1:T(8,128)S(1)} %get-tuple-element.215), channel_id=1, source_target_pairs={{0,1},{1,2},{2,3},{3,4},{4,5},{5,6},{6,7},{7,8},{8,9},{9,10},{10,1... | collective-permute-start | bytes 16640 | tf_op jit(solution)/shard_map/ppermute | solution.py:22
  261.6 14.6 %collective-permute-start.19 = (f32[21,22,3]{2,0,1:T(8,128)S(1)}, f32[21,22,3]{2,0,1:T(8,128)S(1)}, u32[]{:S(2)}, u32[]{:S(2)}) collective-permute-start(f32[21,22,3]{2,0,1:T(8,128)S(1)} %get-tuple-element.216), channel_id=1, source_target_pairs={{1,0},{2,1},{3,2},{4,3},{5,4},{6,5},{7,6},{8,7},{9,8},{10,9},{11,1... | collective-permute-start | bytes 16640 | tf_op jit(solution)/shard_map/ppermute | solution.py:25
  (152 other events, 6748.9 us)
where the time goes:
time: 319 us; the launch traced here: 314 us
  other arithmetic  84.1 us (26%)
  blocking collectives  81.1 us (25%)
  starting transfers between devices  67.7 us (21%)
  waiting for transfers between devices  59.5 us (19%)
  local copies, waits for them, and re-layouts  14.4 us (5%)
  between operations  3.99 us (1%)
  matrix products  3.54 us (1%)
    psum x1, blocking collectives, on_device(): lax.psum(compat_sum, ('rows', 'cols')) / math.sqrt(total_pixels)  81.1 us
    ppermute x10, starting transfers between devices, with_halo(): lax.ppermute(lax.slice_in_dim(block, block.shape[dim] - width, None, axis...  40.5 us
    ppermute x10, waiting for transfers between devices, with_halo(): lax.ppermute(lax.slice_in_dim(block, 0, width, axis=dim), axis, backward)  31.4 us
    ppermute x10, waiting for transfers between devices, with_halo(): lax.ppermute(lax.slice_in_dim(block, block.shape[dim] - width, None, axis...  28.1 us
    ppermute x10, starting transfers between devices, with_halo(): lax.ppermute(lax.slice_in_dim(block, 0, width, axis=dim), axis, backward)  27.2 us
    reduce_sum x16, other arithmetic, pair_terms(): jnp.sum(grad_center * prob_shift + grad_shift * prob_center, axis=0)  16.8 us
    mul x24, other arithmetic, affinity(): spatial_weight(row_step, col_step) * jnp.exp(-distance * factor)  14 us
    sub x1, other arithmetic, softmax_grad(): return prob * (cotangent - jnp.sum(cotangent * prob, axis=0, keepdims=True))  13.9 us
  transfers between devices with their start and end apart: 20, of which 11 were waited for; matrix products, arithmetic and copies ran while one was open for 4% of the time, Pallas kernels for 0%

commit v1 on v0

--- a/solution.py
+++ b/solution.py
@@ -153,7 +153,9 @@
         coefs = coefs + pair_terms(grad_wide, prob_wide)
     unary_grad = unary_sum + softmax_grad(prob_list[0], cotangent)
     feature_grad = feature_term(coefs, kernel_at(), feat_wide)
-    compat_grad = lax.psum(compat_sum, ("rows", "cols")) / math.sqrt(total_pixels)
+    compat_grad = jnp.sum(lax.all_gather(compat_sum, ("rows", "cols")), axis=0) / math.sqrt(
+        total_pixels
+    )
     return (unary_grad, feature_grad, compat_grad)
 
 

time: 319 us -> 948 us (2.97)
  the two profiles are of different devices: /device:TPU:33 before, /device:TPU:16 now
where the time goes in v1:
time: 948 us; the launch traced here: 944 us
  blocking collectives  677 us (71%)
  other arithmetic  88.1 us (9%)
  starting transfers between devices  60.6 us (6%)
  waiting for transfers between devices  60 us (6%)
  local copies, waits for them, and re-layouts  50.7 us (5%)
    all_gather x1, blocking collectives, on_device(): lax.all_gather(compat_sum, ('rows', 'cols'))  677 us
    unnamed x340, local copies, waits for them, and re-layouts  48.3 us
    ppermute x10, starting transfers between devices, with_halo(): lax.ppermute(lax.slice_in_dim(block, block.shape[dim] - width, None, axis...  38.3 us
    ppermute x10, waiting for transfers between devices, with_halo(): lax.ppermute(lax.slice_in_dim(block, 0, width, axis=dim), axis, backward)  32.3 us
    ppermute x10, waiting for transfers between devices, with_halo(): lax.ppermute(lax.slice_in_dim(block, block.shape[dim] - width, None, axis...  27.7 us
    ppermute x10, starting transfers between devices, with_halo(): lax.ppermute(lax.slice_in_dim(block, 0, width, axis=dim), axis, backward)  22.3 us
  transfers between devices with their start and end apart: 20, of which 11 were waited for; matrix products, arithmetic and copies ran while one was open for 5% of the time, Pallas kernels for 0%

profile of v1, /device:TPU:16, one launch (start us, length us, event | category | flops | bytes accessed | tf_op | source)
XLA Modules:
  0.0 943.5 jit_solution(16974011498606952358)
XLA Ops:
  7.8 4.1 collective-permute-start
  13.4 3.9 collective-permute-start.5
  17.3 3.5 collective-permute-start.7
  20.8 11.1 %collective-permute-done.5 = f32[21,22,3]{2,0,1:T(8,128)S(1)} collective-permute-done((f32[21,22,3]{2,0,1:T(8,128)S(1)}, f32[21,22,3]{2,0,1:T(8,128)S(1)}, u32[]{:S(2)}, u32[]{:S(2)}) %collective-permute-start.5) | collective-permute-done | bytes 5576 | tf_op jit(solution)/shard_map/ppermute | solution.py:22
  34.5 6.3 collective-permute-start.2
  40.8 7.7 collective-permute-done.6
  48.5 8.3 collective-permute-done.2
  87.8 4.9 collective-permute-done.9
  92.8 3.6 collective-permute-start.10
  96.4 3.9 collective-permute-start.11
  100.3 3.4 collective-permute-done.10
  103.8 4.9 collective-permute-done.11
  115.9 4.3 collective-permute-start.12
  121.5 4.1 collective-permute-done.13
  125.8 4.5 collective-permute-start.14
  136.8 5.9 collective-permute-done.15
  149.5 4.5 add_reduce_fusion.48
  156.9 3.4 collective-permute-start.16
  162.3 677.2 %all-gather.1 = f32[256,21,21]{2,1,0:T(8,128)} all-gather(f32[1,21,21]{2,1,0:T(8,128)S(1)} %fusion.16), channel_id=2, replica_groups=mesh['rows'=16,'cols'=16] {'rows','cols'}, dimensions={0}, use_global_device_ids=true | all-gather | bytes 453348 | tf_op jit(solution)/shard_map/all_gather | solution.py:156
  888.4 4.3 collective-permute-start.18
  892.7 3.7 collective-permute-start.19
  898.7 4.8 collective-permute-done.19
  918.5 14.6 %fusion.7 = f32[21,16,128]{2,0,1:T(8,128)} fusion(f32[21,16,128]{2,0,1:T(8,128)S(1)} %copy-done.10, f32[16,128]{1,0:T(8,128)} %fusion.20, f32[21,16,128]{2,1,0:T(8,128)} %param.7, f32[21,16,128]{2,0,1:T(8,128)} %copy-done.11, f32[16,128]{1,0:T(8,128)} %get-tuple-element.245, f32[16,128]{1,0:T(8,128)S(1)} %copy-done.14, f32[16,128]{1,0:T(8,128)S(1)} %reduce_max.27, ...), kind=kOutput, calls=%fused_computation.55 | output fusion | flops 9205780 | bytes 18972672 | tf_op jit(solution)/shard_map/sub | solution.py:109
  934.7 8.6 multiply_add_fusion
  (449 shorter events, 134.5 us)
Async XLA Ops:
  0.6 82.8 %copy-start = (f32[21,21]{1,0:T(8,128)S(1)}, f32[21,21]{1,0:T(8,128)}, u32[]{:S(2)}) copy-start(f32[21,21]{1,0:T(8,128)} %param.6) | copy-start | bytes 5296
  3.7 9.5 %collective-permute-start.3 = (f32[21,3,128]{2,0,1:T(8,128)S(1)}, f32[21,3,128]{2,0,1:T(8,128)S(1)}, u32[]{:S(2)}, u32[]{:S(2)}) collective-permute-start(f32[21,3,128]{2,0,1:T(8,128)S(1)} %get-tuple-element.241), channel_id=1, source_target_pairs={{0,16},{16,32},{32,48},{48,64},{64,80},{80,96},{96,112},{112,128},... | collective-permute-start | bytes 96776 | tf_op jit(solution)/shard_map/ppermute | solution.py:22
  5.4 7.8 collective-permute-start.4
  7.8 24.3 %collective-permute-start = (bf16[64,3,128]{2,1,0:T(4,128)(2,1)S(1)}, bf16[64,3,128]{2,1,0:T(4,128)(2,1)S(1)}, u32[]{:S(2)}, u32[]{:S(2)}) collective-permute-start(bf16[64,3,128]{2,1,0:T(4,128)(2,1)S(1)} %get-tuple-element.232), channel_id=1, source_target_pairs={{0,16},{16,32},{32,48},{48,64},{64,80},{80,96},{96,112},{112,128},... | collective-permute-start | bytes 147464 | tf_op jit(solution)/shard_map/ppermute | solution.py:22
  11.9 20.2 %collective-permute-start.1 = (bf16[64,3,128]{2,1,0:T(4,128)(2,1)S(1)}, bf16[64,3,128]{2,1,0:T(4,128)(2,1)S(1)}, u32[]{:S(2)}, u32[]{:S(2)}) collective-permute-start(bf16[64,3,128]{2,1,0:T(4,128)(2,1)S(1)} %get-tuple-element.233), channel_id=1, source_target_pairs={{16,0},{32,16},{48,32},{64,48},{80,64},{96,80},{112,96},{128,112},... | collective-permute-start | bytes 147464 | tf_op jit(solution)/shard_map/ppermute | solution.py:25
  13.4 18.5 %collective-permute-start.5 = (f32[21,22,3]{2,0,1:T(8,128)S(1)}, f32[21,22,3]{2,0,1:T(8,128)S(1)}, u32[]{:S(2)}, u32[]{:S(2)}) collective-permute-start(f32[21,22,3]{2,0,1:T(8,128)S(1)} %get-tuple-element.230), channel_id=1, source_target_pairs={{0,1},{1,2},{2,3},{3,4},{4,5},{5,6},{6,7},{7,8},{8,9},{9,10},{10,1... | collective-permute-start | bytes 16640 | tf_op jit(solution)/shard_map/ppermute | solution.py:22
  17.3 14.6 %collective-permute-start.7 = (f32[21,22,3]{2,0,1:T(8,128)S(1)}, f32[21,22,3]{2,0,1:T(8,128)S(1)}, u32[]{:S(2)}, u32[]{:S(2)}) collective-permute-start(f32[21,22,3]{2,0,1:T(8,128)S(1)} %get-tuple-element.231), channel_id=1, source_target_pairs={{1,0},{2,1},{3,2},{4,3},{5,4},{6,5},{7,6},{8,7},{9,8},{10,9},{11,1... | collective-permute-start | bytes 16640 | tf_op jit(solution)/shard_map/ppermute | solution.py:25
  32.5 16.0 %collective-permute-start.6 = (bf16[64,22,3]{2,1,0:T(8,128)(2,1)S(1)}, bf16[64,22,3]{2,1,0:T(8,128)(2,1)S(1)}, u32[]{:S(2)}, u32[]{:S(2)}) collective-permute-start(bf16[64,22,3]{2,1,0:T(8,128)(2,1)S(1)} %get-tuple-element.214), channel_id=1, source_target_pairs={{1,0},{2,1},{3,2},{4,3},{5,4},{6,5},{7,6},{8,7},{9,8},{10,9},{11,1... | collective-permute-start | bytes 25352 | tf_op jit(solution)/shard_map/ppermute | solution.py:25
  34.5 22.4 %collective-permute-start.2 = (bf16[64,22,3]{2,1,0:T(8,128)(2,1)S(1)}, bf16[64,22,3]{2,1,0:T(8,128)(2,1)S(1)}, u32[]{:S(2)}, u32[]{:S(2)}) collective-permute-start(bf16[64,22,3]{2,1,0:T(8,128)(2,1)S(1)} %get-tuple-element.215), channel_id=1, source_target_pairs={{0,1},{1,2},{2,3},{3,4},{4,5},{5,6},{6,7},{7,8},{8,9},{9,10},{10,1... | collective-permute-start | bytes 25352 | tf_op jit(solution)/shard_map/ppermute | solution.py:22
  66.7 82.4 %copy-start.21 = (f32[16,128]{1,0:T(8,128)}, f32[16,128]{1,0:T(8,128)S(1)}, u32[]{:S(2)}) copy-start(f32[16,128]{1,0:T(8,128)S(1)} %get-tuple-element.257) | copy-start | bytes 24580
  66.7 82.4 %copy-start.23 = (f32[16,128]{1,0:T(8,128)}, f32[16,128]{1,0:T(8,128)S(1)}, u32[]{:S(2)}) copy-start(f32[16,128]{1,0:T(8,128)S(1)} %get-tuple-element.258) | copy-start | bytes 24580
  67.5 81.7 %copy-start.25 = (f32[16,128]{1,0:T(8,128)}, f32[16,128]{1,0:T(8,128)S(1)}, u32[]{:S(2)}) copy-start(f32[16,128]{1,0:T(8,128)S(1)} %get-tuple-element.251) | copy-start | bytes 24580
  84.5 3.3 collective-permute-start.8
  86.4 6.2 collective-permute-start.9
  92.8 11.0 %collective-permute-start.10 = (f32[21,22,3]{2,0,1:T(8,128)S(1)}, f32[21,22,3]{2,0,1:T(8,128)S(1)}, u32[]{:S(2)}, u32[]{:S(2)}) collective-permute-start(f32[21,22,3]{2,0,1:T(8,128)S(1)} %get-tuple-element.226), channel_id=1, source_target_pairs={{0,1},{1,2},{2,3},{3,4},{4,5},{5,6},{6,7},{7,8},{8,9},{9,10},{10,1... | collective-permute-start | bytes 16640 | tf_op jit(solution)/shard_map/ppermute | solution.py:22
  96.4 12.3 %collective-permute-start.11 = (f32[21,22,3]{2,0,1:T(8,128)S(1)}, f32[21,22,3]{2,0,1:T(8,128)S(1)}, u32[]{:S(2)}, u32[]{:S(2)}) collective-permute-start(f32[21,22,3]{2,0,1:T(8,128)S(1)} %get-tuple-element.227), channel_id=1, source_target_pairs={{1,0},{2,1},{3,2},{4,3},{5,4},{6,5},{7,6},{8,7},{9,8},{10,9},{11,1... | collective-permute-start | bytes 16640 | tf_op jit(solution)/shard_map/ppermute | solution.py:25
  115.9 5.7 collective-permute-start.12
  120.2 5.4 collective-permute-start.13
  125.8 11.0 %collective-permute-start.14 = (f32[21,22,3]{2,0,1:T(8,128)S(1)}, f32[21,22,3]{2,0,1:T(8,128)S(1)}, u32[]{:S(2)}, u32[]{:S(2)}) collective-permute-start(f32[21,22,3]{2,0,1:T(8,128)S(1)} %get-tuple-element.222), channel_id=1, source_target_pairs={{0,1},{1,2},{2,3},{3,4},{4,5},{5,6},{6,7},{7,8},{8,9},{9,10},{10,1... | collective-permute-start | bytes 16640 | tf_op jit(solution)/shard_map/ppermute | solution.py:22
  130.3 12.3 %collective-permute-start.15 = (f32[21,22,3]{2,0,1:T(8,128)S(1)}, f32[21,22,3]{2,0,1:T(8,128)S(1)}, u32[]{:S(2)}, u32[]{:S(2)}) collective-permute-start(f32[21,22,3]{2,0,1:T(8,128)S(1)} %get-tuple-element.223), channel_id=1, source_target_pairs={{1,0},{2,1},{3,2},{4,3},{5,4},{6,5},{7,6},{8,7},{9,8},{10,9},{11,1... | collective-permute-start | bytes 16640 | tf_op jit(solution)/shard_map/ppermute | solution.py:25
  156.9 731.3 %collective-permute-start.16 = (f32[21,3,128]{2,0,1:T(8,128)S(1)}, f32[21,3,128]{2,0,1:T(8,128)S(1)}, u32[]{:S(2)}, u32[]{:S(2)}) collective-permute-start(f32[21,3,128]{2,0,1:T(8,128)S(1)} %get-tuple-element.235), channel_id=1, source_target_pairs={{0,16},{16,32},{32,48},{48,64},{64,80},{80,96},{96,112},{112,128},... | collective-permute-start | bytes 96776 | tf_op jit(solution)/shard_map/ppermute | solution.py:22
  160.4 727.8 %collective-permute-start.17 = (f32[21,3,128]{2,0,1:T(8,128)S(1)}, f32[21,3,128]{2,0,1:T(8,128)S(1)}, u32[]{:S(2)}, u32[]{:S(2)}) collective-permute-start(f32[21,3,128]{2,0,1:T(8,128)S(1)} %get-tuple-element.236), channel_id=1, source_target_pairs={{16,0},{32,16},{48,32},{64,48},{80,64},{96,80},{112,96},{128,112},... | collective-permute-start | bytes 96776 | tf_op jit(solution)/shard_map/ppermute | solution.py:25
  888.4 10.3 %collective-permute-start.18 = (f32[21,22,3]{2,0,1:T(8,128)S(1)}, f32[21,22,3]{2,0,1:T(8,128)S(1)}, u32[]{:S(2)}, u32[]{:S(2)}) collective-permute-start(f32[21,22,3]{2,0,1:T(8,128)S(1)} %get-tuple-element.218), channel_id=1, source_target_pairs={{0,1},{1,2},{2,3},{3,4},{4,5},{5,6},{6,7},{7,8},{8,9},{9,10},{10,1... | collective-permute-start | bytes 16640 | tf_op jit(solution)/shard_map/ppermute | solution.py:22
  892.7 10.8 %collective-permute-start.19 = (f32[21,22,3]{2,0,1:T(8,128)S(1)}, f32[21,22,3]{2,0,1:T(8,128)S(1)}, u32[]{:S(2)}, u32[]{:S(2)}) collective-permute-start(f32[21,22,3]{2,0,1:T(8,128)S(1)} %get-tuple-element.219), channel_id=1, source_target_pairs={{1,0},{2,1},{3,2},{4,3},{5,4},{6,5},{7,6},{8,7},{9,8},{10,9},{11,1... | collective-permute-start | bytes 16640 | tf_op jit(solution)/shard_map/ppermute | solution.py:25
  (118 other events, 4064.8 us)
